TPU v7x, 32 devices: a whole 2x2x4 slice. The times are simulated.
32 devices in a mesh: ctx: 8 (over z, x), tp: 4 (over y, core).
Axes of the slice: x: 2, y: 2, z: 4, core: 2. Of those that a mesh axis runs over, the one named last changes fastest.
Arguments:
- hidden_input: bfloat16 [256, 8192], P(None, 'ctx'), may hold values from -6 to 6
- w_query: bfloat16 [8192, 8192], P('ctx', 'tp')
- key_value_weight: bfloat16 [8192, 2, 1024], P('ctx', None, 'tp'), may hold values from -0.0625 to 0.0625
- w_out: bfloat16 [8192, 8192], P('tp', 'ctx'), may hold values from -0.0625 to 0.0625
- key_value_cache: bfloat16 [2, 8, 32768, 128], P(None, 'tp', 'ctx'), may hold values from -6 to 6
- filled: int32 [8], P('ctx'), may hold values from 512 to 4096, as said below
- positions: int32 [256], replicated, may hold values from 0 to 255, each once
Outputs:
- layer_out: bfloat16 [256, 8192], P('tp', 'ctx')
Inputs may be any that keep to these rules, and one draw needn't show every extreme that they name: `filled`: every shard has at least 512 used slots; some shard is full and some holds exactly 512.
All inputs are finite; a program needn't handle non-finite values.
Results may differ from a plain program's by a relative error of at most 0.0045.
The roundings to bfloat16 on the way count: a program that leaves them out, or rounds other values in their place, can miss the bound.
Values may be sent and summed in bfloat16 or wider, within the bound.
A program may use at most 128 MiB of HBM per device.

v0:
```python
import math
import jax
import jax.numpy as jnp
from jax import lax
from jax.sharding import PartitionSpec as P

NEG_FILL = -1e30


def cache_attend(query_rows, key_rows, val_rows, filled_now, inv_root):
    slots = key_rows.shape[1]
    block = math.gcd(slots, 1024)
    blocks = slots // block

    def block_step(block_idx, carry):
        row_max, denom, accum = carry
        key_block = lax.dynamic_slice_in_dim(key_rows, block_idx * block, block, 1)
        val_block = lax.dynamic_slice_in_dim(val_rows, block_idx * block, block, 1)
        scores = (
            jnp.einsum("kgrd,ksd->kgrs", query_rows, key_block, preferred_element_type=jnp.float32)
            * inv_root
        )
        places = block_idx * block + jnp.arange(block, dtype=jnp.int32)
        scores = jnp.where(places < filled_now, scores, NEG_FILL)
        new_max = jnp.maximum(row_max, jnp.max(scores, axis=-1))
        rescale = jnp.exp(row_max - new_max)
        probs = jnp.exp(scores - new_max[..., None])
        update = jnp.einsum(
            "kgrs,ksd->kgrd",
            probs.astype(jnp.bfloat16),
            val_block,
            preferred_element_type=jnp.float32,
        )
        accum = accum * rescale[..., None] + update
        denom = denom * rescale + jnp.sum(probs, axis=-1)
        return (new_max, denom, accum)

    start = (
        jnp.full(query_rows.shape[:3], NEG_FILL, jnp.float32),
        jnp.zeros(query_rows.shape[:3], jnp.float32),
        jnp.zeros(query_rows.shape, jnp.float32),
    )
    row_max, denom, accum = lax.fori_loop(0, blocks, block_step, start)
    return (row_max + jnp.log(denom), accum / denom[..., None])


def block_attend(query_rows, key_rows, val_rows, causal_mask, inv_root):
    scores = (
        jnp.einsum("kgrd,ksd->kgrs", query_rows, key_rows, preferred_element_type=jnp.float32)
        * inv_root
    )
    scores = jnp.where(causal_mask[None, None], scores, NEG_FILL)
    row_max = jnp.max(scores, axis=-1)
    probs = jnp.exp(scores - row_max[..., None])
    denom = jnp.sum(probs, axis=-1)
    accum = jnp.einsum(
        "kgrs,ksd->kgrd", probs.astype(jnp.bfloat16), val_rows, preferred_element_type=jnp.float32
    )
    return (row_max + jnp.log(denom), accum / denom[..., None])


def to_tokens(log_sums, outputs):
    row_count = log_sums.shape[2]
    head_dim = outputs.shape[3]
    return (
        log_sums.reshape(-1, row_count).T,
        jnp.transpose(outputs.reshape(-1, row_count, head_dim), (1, 0, 2)),
    )


def body(hidden_input, w_query, key_value_weight, w_out, key_value_cache, filled, positions):
    tokens = hidden_input.shape[0]
    shards = lax.axis_size("ctx")
    own_rows = tokens // shards
    kv_heads = key_value_cache.shape[1]
    head_dim = key_value_cache.shape[3]
    q_heads = w_query.shape[1] // head_dim
    group_size = q_heads // kv_heads
    width_loc = w_query.shape[0]
    inv_root = 1.0 / math.sqrt(head_dim)
    w_in = jnp.concatenate([w_query, key_value_weight.reshape(width_loc, -1)], axis=1)
    projected_all = lax.psum(
        jnp.dot(hidden_input, w_in, preferred_element_type=jnp.float32), "ctx"
    ).astype(jnp.bfloat16)
    query_cols = q_heads * head_dim
    kv_cols = kv_heads * head_dim
    query_rows = jnp.transpose(
        projected_all[:, :query_cols].reshape(tokens, kv_heads, group_size, head_dim), (1, 2, 0, 3)
    )
    new_keys = jnp.transpose(
        projected_all[:, query_cols : query_cols + kv_cols].reshape(tokens, kv_heads, head_dim),
        (1, 0, 2),
    )
    new_vals = jnp.transpose(
        projected_all[:, query_cols + kv_cols :].reshape(tokens, kv_heads, head_dim), (1, 0, 2)
    )
    cache_log, cache_out = to_tokens(
        *cache_attend(query_rows, key_value_cache[0], key_value_cache[1], filled[0], inv_root)
    )
    log_parts, out_parts = (
        lax.all_to_all(cache_log[None], "ctx", split_axis=1, concat_axis=0, tiled=True),
        lax.all_to_all(cache_out[None], "ctx", split_axis=1, concat_axis=0, tiled=True),
    )
    first_own = lax.axis_index("ctx") * own_rows
    own_queries = lax.dynamic_slice_in_dim(query_rows, first_own, own_rows, 2)
    own_positions = lax.dynamic_slice_in_dim(positions, first_own, own_rows, 0)
    causal_mask = positions[None, :] <= own_positions[:, None]
    new_log, new_out = to_tokens(
        *block_attend(own_queries, new_keys, new_vals, causal_mask, inv_root)
    )
    all_log = jnp.concatenate([log_parts, new_log[None]], axis=0)
    all_out = jnp.concatenate([out_parts, new_out[None]], axis=0)
    top_log = jnp.max(all_log, axis=0)
    shares = jnp.exp(all_log - top_log[None])
    merged = jnp.sum(shares[..., None] * all_out, axis=0) / jnp.sum(shares, axis=0)[..., None]
    attended = merged.astype(jnp.bfloat16).reshape(own_rows, query_cols)
    part_out = jnp.dot(
        lax.all_gather(attended, "ctx", axis=0, tiled=True),
        w_out,
        preferred_element_type=jnp.float32,
    )
    return lax.psum_scatter(part_out, "tp", scatter_dimension=0, tiled=True).astype(jnp.bfloat16)


def solution(mesh):
    placed = (
        P(None, "ctx"),
        P("ctx", "tp"),
        P("ctx", None, "tp"),
        P("tp", "ctx"),
        P(None, "tp", "ctx", None),
        P("ctx"),
        P(),
    )
    return jax.shard_map(
        body, mesh=mesh, in_specs=placed, out_specs=P("tp", "ctx"), check_vma=False
    )
```

profile of v0, /device:TPU:0, one launch (start us, length us, event | category | flops | bytes accessed | tf_op | source)
XLA Modules:
  0.0 340.0 jit_solution(6594446714789034644)
XLA Ops:
  8.1 5.3 %fusion.23 = f32[256,2560]{0,1:T(8,128)} fusion(bf16[256,1024]{1,0:T(8,128)(2,1)S(1)} %copy-done, bf16[1024,512]{1,0:T(8,128)(2,1)S(1)} %bitcast.114, bf16[1024,2048]{1,0:T(8,128)(2,1)} %param.10), kind=kOutput, calls=%fused_computation.28 | convolution fusion | flops 1352663040 | bytes 8388608 | tf_op jit(solution)/shard_map/dot_general | solution.py:83
  13.4 109.1 %all-reduce.1 = bf16[256,2560]{0,1:T(8,128)(2,1)S(1)} all-reduce(f32[256,2560]{0,1:T(8,128)} %fusion.23), channel_id=1, replica_groups=mesh['ctx'=8,'tp'=4] {'ctx'}, use_global_device_ids=true, to_apply=%region_0.0 | all-reduce | flops 655360 | bytes 3932160 | tf_op jit(solution)/shard_map/psum | solution.py:82
  125.1 4.4 %slice_bitcast_fusion = (bf16[2,4096,128]{2,1,0:T(8,128)(2,1)}, bf16[2,4096,128]{2,1,0:T(8,128)(2,1)}) fusion(bf16[2,2,4096,128]{3,2,1,0:T(8,128)(2,1)} %param.13), kind=kLoop, calls=%fused_computation.32 | loop fusion | bytes 8388608 | tf_op jit(solution)/shard_map/squeeze | solution.py:98
  129.5 66.4 %while.18 = (s32[]{:T(128)}, f32[2,8,256]{2,1,0:T(8,128)S(1)}, f32[2,8,256]{2,1,0:T(8,128)S(1)}, f32[2,8,256,128]{3,2,1,0:T(8,128)}, s32[]{:T(128)}, /*index=5*/...) while((s32[]{:T(128)}, f32[2,8,256]{2,1,0:T(8,128)S(1)}, ...), condition=%wide.region_4.5_spmd.clone, body=%wide.region_1.4_spmd.clone.sunk | while | flops 2195216384 | bytes 73666816 | solution.py:43
  130.2 3.8 %bitcast_reduce_fusion.2 = (f32[2,8,256]{2,1,0:T(8,128)S(1)}, f32[2,1024,8,256]{3,1,2,0:T(8,128)S(1)}) fusion(pred[1024]{0:T(1024)(128)(4,1)S(1)} %add_compare_fusion.2, bf16[2,8,256,128]{3,2,1,0:T(8,128)(2,1)S(1)} %get-tuple-element.291, bf16[2,4096,128]{2,1,0:T(8,128)(2,1)} %get-tuple-element.290, s32[]{:T(128)S(6)} %select_n.52), kind=kOutput, calls=%fused_computation.1.clone.1 | convolution fusion | flops 1086320640 | bytes 18367492 | tf_op jit(solution)/shard_map/while/body/eval_jaxpr/kgrd,ksd->kgrs/dot_general | solution.py:20
  134.0 4.1 %fusion.58 = f32[2,8,256]{2,1,0:T(8,128)S(1)} fusion(f32[2,1024,8,256]{3,1,2,0:T(8,128)S(1)} %get-tuple-element.258, f32[2,8,256]{2,1,0:T(8,128)S(1)} %select_maximum_fusion.2, pred[1024]{0:T(1024)(128)(4,1)S(1)} %add_compare_fusion.2), kind=kLoop, calls=%fused_computation.5.clone.1 | loop fusion | flops 16773120 | bytes 16811008 | tf_op jit(solution)/shard_map/while/body/eval_jaxpr/reduce_sum | solution.py:35
  138.1 6.7 %fusion.60 = f32[2,8,256,128]{3,2,1,0:T(8,128)S(1)} fusion(f32[2,8,256,128]{3,2,1,0:T(8,128)S(1)} %copy-done.1, f32[2,1024,8,256]{3,1,2,0:T(8,128)S(1)} %get-tuple-element.258, f32[2,8,256]{2,1,0:T(8,128)S(1)} %select_maximum_fusion.2, pred[1024]{0:T(1024)(128)(4,1)S(1)} %add_compare_fusion.2, f32[2,8,256]{2,1,0:T(8,128)S(1)} %get-tuple-element.260, ...), kind=kOutput, calls=%fused_computation.9.clone.1 | convolution fusion | flops 1092091904 | bytes 21529604 | tf_op jit(solution)/shard_map/while/body/eval_jaxpr/kgrs,ksd->kgrd/dot_general | solution.py:28
  146.8 3.8 %bitcast_reduce_fusion.2 = (f32[2,8,256]{2,1,0:T(8,128)S(1)}, f32[2,1024,8,256]{3,1,2,0:T(8,128)S(1)}) fusion(pred[1024]{0:T(1024)(128)(4,1)S(1)} %add_compare_fusion.2, bf16[2,8,256,128]{3,2,1,0:T(8,128)(2,1)S(1)} %get-tuple-element.291, bf16[2,4096,128]{2,1,0:T(8,128)(2,1)} %get-tuple-element.290, s32[]{:T(128)S(6)} %select_n.52), kind=kOutput, calls=%fused_computation.1.clone.1 | convolution fusion | flops 1086320640 | bytes 18367492 | tf_op jit(solution)/shard_map/while/body/eval_jaxpr/kgrd,ksd->kgrs/dot_general | solution.py:20
  150.6 4.1 %fusion.58 = f32[2,8,256]{2,1,0:T(8,128)S(1)} fusion(f32[2,1024,8,256]{3,1,2,0:T(8,128)S(1)} %get-tuple-element.258, f32[2,8,256]{2,1,0:T(8,128)S(1)} %select_maximum_fusion.2, pred[1024]{0:T(1024)(128)(4,1)S(1)} %add_compare_fusion.2), kind=kLoop, calls=%fused_computation.5.clone.1 | loop fusion | flops 16773120 | bytes 16811008 | tf_op jit(solution)/shard_map/while/body/eval_jaxpr/reduce_sum | solution.py:35
  154.7 6.7 %fusion.60 = f32[2,8,256,128]{3,2,1,0:T(8,128)S(1)} fusion(f32[2,8,256,128]{3,2,1,0:T(8,128)S(1)} %copy-done.1, f32[2,1024,8,256]{3,1,2,0:T(8,128)S(1)} %get-tuple-element.258, f32[2,8,256]{2,1,0:T(8,128)S(1)} %select_maximum_fusion.2, pred[1024]{0:T(1024)(128)(4,1)S(1)} %add_compare_fusion.2, f32[2,8,256]{2,1,0:T(8,128)S(1)} %get-tuple-element.260, ...), kind=kOutput, calls=%fused_computation.9.clone.1 | convolution fusion | flops 1092091904 | bytes 21529604 | tf_op jit(solution)/shard_map/while/body/eval_jaxpr/kgrs,ksd->kgrd/dot_general | solution.py:28
  163.4 3.8 %bitcast_reduce_fusion.2 = (f32[2,8,256]{2,1,0:T(8,128)S(1)}, f32[2,1024,8,256]{3,1,2,0:T(8,128)S(1)}) fusion(pred[1024]{0:T(1024)(128)(4,1)S(1)} %add_compare_fusion.2, bf16[2,8,256,128]{3,2,1,0:T(8,128)(2,1)S(1)} %get-tuple-element.291, bf16[2,4096,128]{2,1,0:T(8,128)(2,1)} %get-tuple-element.290, s32[]{:T(128)S(6)} %select_n.52), kind=kOutput, calls=%fused_computation.1.clone.1 | convolution fusion | flops 1086320640 | bytes 18367492 | tf_op jit(solution)/shard_map/while/body/eval_jaxpr/kgrd,ksd->kgrs/dot_general | solution.py:20
  167.2 4.1 %fusion.58 = f32[2,8,256]{2,1,0:T(8,128)S(1)} fusion(f32[2,1024,8,256]{3,1,2,0:T(8,128)S(1)} %get-tuple-element.258, f32[2,8,256]{2,1,0:T(8,128)S(1)} %select_maximum_fusion.2, pred[1024]{0:T(1024)(128)(4,1)S(1)} %add_compare_fusion.2), kind=kLoop, calls=%fused_computation.5.clone.1 | loop fusion | flops 16773120 | bytes 16811008 | tf_op jit(solution)/shard_map/while/body/eval_jaxpr/reduce_sum | solution.py:35
  171.3 6.7 %fusion.60 = f32[2,8,256,128]{3,2,1,0:T(8,128)S(1)} fusion(f32[2,8,256,128]{3,2,1,0:T(8,128)S(1)} %copy-done.1, f32[2,1024,8,256]{3,1,2,0:T(8,128)S(1)} %get-tuple-element.258, f32[2,8,256]{2,1,0:T(8,128)S(1)} %select_maximum_fusion.2, pred[1024]{0:T(1024)(128)(4,1)S(1)} %add_compare_fusion.2, f32[2,8,256]{2,1,0:T(8,128)S(1)} %get-tuple-element.260, ...), kind=kOutput, calls=%fused_computation.9.clone.1 | convolution fusion | flops 1092091904 | bytes 21529604 | tf_op jit(solution)/shard_map/while/body/eval_jaxpr/kgrs,ksd->kgrd/dot_general | solution.py:28
  180.0 3.8 %bitcast_reduce_fusion.2 = (f32[2,8,256]{2,1,0:T(8,128)S(1)}, f32[2,1024,8,256]{3,1,2,0:T(8,128)S(1)}) fusion(pred[1024]{0:T(1024)(128)(4,1)S(1)} %add_compare_fusion.2, bf16[2,8,256,128]{3,2,1,0:T(8,128)(2,1)S(1)} %get-tuple-element.291, bf16[2,4096,128]{2,1,0:T(8,128)(2,1)} %get-tuple-element.290, s32[]{:T(128)S(6)} %select_n.52), kind=kOutput, calls=%fused_computation.1.clone.1 | convolution fusion | flops 1086320640 | bytes 18367492 | tf_op jit(solution)/shard_map/while/body/eval_jaxpr/kgrd,ksd->kgrs/dot_general | solution.py:20
  183.8 4.1 %fusion.58 = f32[2,8,256]{2,1,0:T(8,128)S(1)} fusion(f32[2,1024,8,256]{3,1,2,0:T(8,128)S(1)} %get-tuple-element.258, f32[2,8,256]{2,1,0:T(8,128)S(1)} %select_maximum_fusion.2, pred[1024]{0:T(1024)(128)(4,1)S(1)} %add_compare_fusion.2), kind=kLoop, calls=%fused_computation.5.clone.1 | loop fusion | flops 16773120 | bytes 16811008 | tf_op jit(solution)/shard_map/while/body/eval_jaxpr/reduce_sum | solution.py:35
  187.9 6.7 %fusion.60 = f32[2,8,256,128]{3,2,1,0:T(8,128)S(1)} fusion(f32[2,8,256,128]{3,2,1,0:T(8,128)S(1)} %copy-done.1, f32[2,1024,8,256]{3,1,2,0:T(8,128)S(1)} %get-tuple-element.258, f32[2,8,256]{2,1,0:T(8,128)S(1)} %select_maximum_fusion.2, pred[1024]{0:T(1024)(128)(4,1)S(1)} %add_compare_fusion.2, f32[2,8,256]{2,1,0:T(8,128)S(1)} %get-tuple-element.260, ...), kind=kOutput, calls=%fused_computation.9.clone.1 | convolution fusion | flops 1092091904 | bytes 21529604 | tf_op jit(solution)/shard_map/while/body/eval_jaxpr/kgrs,ksd->kgrd/dot_general | solution.py:28
  198.2 3.5 %all-to-all-start = ((f32[8,1,512]{2,1,0:T(1,128)}), f32[8,1,512]{2,1,0:T(1,128)S(1)}, u32[]{:S(2)}, u32[]{:S(2)}) async-start(f32[8,1,512]{2,1,0:T(1,128)} %reshape.106), calls=%async_computation | async-start | bytes 32768 | tf_op jit(solution)/shard_map/all_to_all | solution.py:101
  203.6 2.5 copy.69
  208.3 4.3 %all-to-all-start.1 = ((f32[1,256,16,128]{3,2,0,1:T(8,128)}), f32[1,256,16,128]{3,2,0,1:T(8,128)}, u32[]{:S(2)}, u32[]{:S(2)}) async-start(f32[1,256,16,128]{3,2,0,1:T(8,128)} %bitcast.109), calls=%async_computation.1 | async-start | bytes 4194304 | tf_op jit(solution)/shard_map/all_to_all | solution.py:102
  215.3 44.4 %all-to-all-done.1 = f32[1,256,16,128]{3,2,0,1:T(8,128)} async-done(((f32[1,256,16,128]{3,2,0,1:T(8,128)}), f32[1,256,16,128]{3,2,0,1:T(8,128)}, u32[]{:S(2)}, u32[]{:S(2)}) %all-to-all-start.1) | async-done | bytes 2097184 | tf_op jit(solution)/shard_map/all_to_all | solution.py:102
  259.6 2.3 copy.58
  263.6 39.3 %all-gather.2.cloned.1.call-done = bf16[256,2048]{1,0:T(8,128)(2,1)} async-done(((bf16[32,2048]{1,0:T(8,128)(2,1)}), bf16[256,2048]{1,0:T(8,128)(2,1)}) %all-gather.2.cloned.1.call-update) | async-done | bytes 1048592 | tf_op jit(solution)/shard_map/all_gather | solution.py:118
  302.9 4.8 %fusion.43 = f32[256,1024]{1,0:T(8,128)} fusion(bf16[256,2048]{1,0:T(8,128)(2,1)} %all-gather.2.cloned.1.call-done, bf16[2048,1024]{1,0:T(8,128)(2,1)} %param.12), kind=kOutput, calls=%fused_computation.60 | convolution fusion | flops 1073741824 | bytes 6291456 | tf_op jit(solution)/shard_map/dot_general | solution.py:117
  307.7 23.8 %reduce-scatter.2.cloned.1.call-done = f32[64,1024]{1,0:T(8,128)} async-done(((f32[256,1024]{1,0:T(8,128)}), f32[64,1024]{1,0:T(8,128)}) %reduce-scatter.2.cloned.1.call-update) | async-done | bytes 262160 | tf_op jit(solution)/shard_map/reduce_scatter | solution.py:122
  (74 shorter events, 24.3 us)
Async XLA Ops:
  6.5 1.5 copy-start
  134.0 4.1 %copy-start.1 = (f32[2,8,256,128]{3,2,1,0:T(8,128)S(1)}, f32[2,8,256,128]{3,2,1,0:T(8,128)}, u32[]{:S(2)}) copy-start(f32[2,8,256,128]{3,2,1,0:T(8,128)} %get-tuple-element.276) | copy-start | bytes 6291460 | tf_op jit(solution)/shard_map/while
  144.8 1.3 copy-start.2
  150.6 4.1 %copy-start.1 = (f32[2,8,256,128]{3,2,1,0:T(8,128)S(1)}, f32[2,8,256,128]{3,2,1,0:T(8,128)}, u32[]{:S(2)}) copy-start(f32[2,8,256,128]{3,2,1,0:T(8,128)} %get-tuple-element.276) | copy-start | bytes 6291460 | tf_op jit(solution)/shard_map/while
  161.4 1.3 copy-start.2
  167.2 4.1 %copy-start.1 = (f32[2,8,256,128]{3,2,1,0:T(8,128)S(1)}, f32[2,8,256,128]{3,2,1,0:T(8,128)}, u32[]{:S(2)}) copy-start(f32[2,8,256,128]{3,2,1,0:T(8,128)} %get-tuple-element.276) | copy-start | bytes 6291460 | tf_op jit(solution)/shard_map/while
  178.0 1.3 copy-start.2
  183.8 4.1 %copy-start.1 = (f32[2,8,256,128]{3,2,1,0:T(8,128)S(1)}, f32[2,8,256,128]{3,2,1,0:T(8,128)}, u32[]{:S(2)}) copy-start(f32[2,8,256,128]{3,2,1,0:T(8,128)} %get-tuple-element.276) | copy-start | bytes 6291460 | tf_op jit(solution)/shard_map/while
  194.6 1.3 copy-start.2
  198.2 10.1 %all-to-all-start = ((f32[8,1,512]{2,1,0:T(1,128)}), f32[8,1,512]{2,1,0:T(1,128)S(1)}, u32[]{:S(2)}, u32[]{:S(2)}) async-start(f32[8,1,512]{2,1,0:T(1,128)} %reshape.106), calls=%async_computation | async-start | bytes 32768 | tf_op jit(solution)/shard_map/all_to_all | solution.py:101
  203.6 9.3 %copy-start.3 = (s32[256]{0:T(256)S(1)}, s32[256]{0:T(256)}, u32[]{:S(2)}) copy-start(s32[256]{0:T(256)} %param.15) | copy-start | bytes 3076
  208.3 51.4 %all-to-all-start.1 = ((f32[1,256,16,128]{3,2,0,1:T(8,128)}), f32[1,256,16,128]{3,2,0,1:T(8,128)}, u32[]{:S(2)}, u32[]{:S(2)}) async-start(f32[1,256,16,128]{3,2,0,1:T(8,128)} %bitcast.109), calls=%async_computation.1 | async-start | bytes 4194304 | tf_op jit(solution)/shard_map/all_to_all | solution.py:102
  212.6 90.3 %all-gather.2.cloned.1.call-start = ((), (), s32[]{:S(2)}) async-start(), calls=%async_computation.3 | async-start | bytes 1179648 | tf_op jit(solution)/shard_map/all_gather | solution.py:118
  263.5 68.0 %reduce-scatter.2.cloned.1.call-start = ((), (), s32[]{:S(2)}) async-start(), calls=%async_computation.4 | async-start | bytes 1310720 | tf_op jit(solution)/shard_map/reduce_scatter | solution.py:122
Sparse Core Ops, SparseCore 0:
  263.7 39.2 all-gather.1
  307.8 23.6 reduce-scatter.1
where the time goes:
time: 341 us; the launch traced here: 340 us
  waiting for transfers between devices  110 us (32%)
  blocking collectives  109 us (32%)
  matrix products  52.4 us (15%)
  other arithmetic  26.1 us (8%)
  local copies, waits for them, and re-layouts  20.9 us (6%)
  between operations  13.6 us (4%)
  starting transfers between devices  7.95 us (2%)
    psum x1, blocking collectives, body(): lax.psum(jnp.dot(hidden_input, w_in, preferred_element_type=jnp.float32),...  109 us
    all_to_all x1, waiting for transfers between devices, body(): lax.all_to_all(cache_out[None], 'ctx', split_axis=1, concat_axis=0, tiled...  44.4 us
    all_gather x1, waiting for transfers between devices, body(): lax.all_gather(attended, 'ctx', axis=0, tiled=True)  39.3 us
    dot_general x4, matrix products, block_step(): jnp.einsum('kgrs,ksd->kgrd', probs.astype(jnp.bfloat16), val_block, prefe...  26.7 us
    reduce_scatter x1, waiting for transfers between devices, body(): lax.psum_scatter(part_out, 'tp', scatter_dimension=0, tiled=True)  23.8 us
    reduce_sum x4, other arithmetic, block_step(): denom = denom * rescale + jnp.sum(probs, axis=-1)  16.3 us
    dot_general x4, matrix products, block_step(): jnp.einsum('kgrd,ksd->kgrs', query_rows, key_block, preferred_element_typ...  15.1 us
  transfers between devices with their start and end apart: 4, of which 4 were waited for; matrix products, arithmetic and copies ran while one was open for 2% of the time, Pallas kernels for 0%

commit v1 on v0

--- a/solution.py
+++ b/solution.py
@@ -3,8 +3,25 @@
 import jax.numpy as jnp
 from jax import lax
 from jax.sharding import PartitionSpec as P
+from jax.lax import axis_index, axis_size, ppermute
 
 NEG_FILL = -1e30
+
+
+def rails_read(x_part, array_dim):
+    axis_name = "ctx"
+    extra = axis_index(axis_name)
+    out_arr = axis_size(axis_name)
+    high, latest, x_now = (out_arr, extra, x_part.shape[array_dim])
+    u1, d_next = (x_part, 1)
+    while d_next < high:
+        trail = []
+        for h in tuple(range(high)):
+            trail.append((h, (h - d_next) % high))
+        z1 = ppermute(u1, axis_name, trail)
+        u1 = jnp.concatenate([u1, z1], array_dim)
+        d_next = 2 * d_next
+    return jnp.roll(u1, latest * x_now, array_dim)
 
 
 def cache_attend(query_rows, key_rows, val_rows, filled_now, inv_root):
@@ -114,11 +131,7 @@
     shares = jnp.exp(all_log - top_log[None])
     merged = jnp.sum(shares[..., None] * all_out, axis=0) / jnp.sum(shares, axis=0)[..., None]
     attended = merged.astype(jnp.bfloat16).reshape(own_rows, query_cols)
-    part_out = jnp.dot(
-        lax.all_gather(attended, "ctx", axis=0, tiled=True),
-        w_out,
-        preferred_element_type=jnp.float32,
-    )
+    part_out = jnp.dot(rails_read(attended, 0), w_out, preferred_element_type=jnp.float32)
     return lax.psum_scatter(part_out, "tp", scatter_dimension=0, tiled=True).astype(jnp.bfloat16)
 
 

time: 341 us -> 339 us (level)
  starting transfers between devices: 7.95 us -> 12.2 us
  waiting for transfers between devices: 110 us -> 106 us
    all_gather x1 -> x0, waiting for transfers between devices: 39.3 us -> none  [body(): lax.all_gather(attended, 'ctx', axis=0, tiled=True)]
    ppermute x0 -> x3, waiting for transfers between devices: none -> 32.7 us  [rails_read(): z1 = ppermute(u1, axis_name, trail)]
    ppermute x0 -> x3, starting transfers between devices: none -> 4.14 us  [rails_read(): z1 = ppermute(u1, axis_name, trail)]
  transfers between devices with their start and end apart: 4 -> 6, of which waited for: 4 -> 6; matrix products, arithmetic and copies ran while one was open for 2% -> 2% of each run, Pallas kernels for 0% -> 0%
where the time goes in v1:
time: 339 us; the launch traced here: 338 us
  blocking collectives  109 us (32%)
  waiting for transfers between devices  106 us (31%)
  matrix products  49.9 us (15%)
  other arithmetic  25.8 us (8%)
  local copies, waits for them, and re-layouts  21 us (6%)
  between operations  13.7 us (4%)
  starting transfers between devices  12.2 us (4%)
    psum x1, blocking collectives, body(): lax.psum(jnp.dot(hidden_input, w_in, preferred_element_type=jnp.float32),...  109 us
    all_to_all x1, waiting for transfers between devices, body(): lax.all_to_all(cache_out[None], 'ctx', split_axis=1, concat_axis=0, tiled...  44.3 us
    ppermute x3, waiting for transfers between devices, rails_read(): z1 = ppermute(u1, axis_name, trail)  32.7 us
    reduce_scatter x1, waiting for transfers between devices, body(): lax.psum_scatter(part_out, 'tp', scatter_dimension=0, tiled=True)  26.9 us
    dot_general x4, matrix products, block_step(): jnp.einsum('kgrs,ksd->kgrd', probs.astype(jnp.bfloat16), val_block, prefe...  26.7 us
    reduce_sum x4, other arithmetic, block_step(): denom = denom * rescale + jnp.sum(probs, axis=-1)  16.3 us
    dot_general x4, matrix products, block_step(): jnp.einsum('kgrd,ksd->kgrs', query_rows, key_block, preferred_element_typ...  15.1 us
  transfers between devices with their start and end apart: 6, of which 6 were waited for; matrix products, arithmetic and copies ran while one was open for 2% of the time, Pallas kernels for 0%

profile of v1, /device:TPU:0, one launch (start us, length us, event | category | flops | bytes accessed | tf_op | source)
XLA Modules:
  0.0 338.1 jit_solution(17550801999106035414)
XLA Ops:
  8.1 5.3 %fusion.23 = f32[256,2560]{0,1:T(8,128)} fusion(bf16[256,1024]{1,0:T(8,128)(2,1)S(1)} %copy-done, bf16[1024,512]{1,0:T(8,128)(2,1)S(1)} %bitcast.119, bf16[1024,2048]{1,0:T(8,128)(2,1)} %param.10), kind=kOutput, calls=%fused_computation.28 | convolution fusion | flops 1352663040 | bytes 8388608 | tf_op jit(solution)/shard_map/dot_general | solution.py:100
  13.4 109.1 %all-reduce.1 = bf16[256,2560]{0,1:T(8,128)(2,1)S(1)} all-reduce(f32[256,2560]{0,1:T(8,128)} %fusion.23), channel_id=1, replica_groups=mesh['ctx'=8,'tp'=4] {'ctx'}, use_global_device_ids=true, to_apply=%region_0.0 | all-reduce | flops 655360 | bytes 3932160 | tf_op jit(solution)/shard_map/psum | solution.py:99
  125.1 4.4 %slice_bitcast_fusion = (bf16[2,4096,128]{2,1,0:T(8,128)(2,1)}, bf16[2,4096,128]{2,1,0:T(8,128)(2,1)}) fusion(bf16[2,2,4096,128]{3,2,1,0:T(8,128)(2,1)} %param.13), kind=kLoop, calls=%fused_computation.32 | loop fusion | bytes 8388608 | tf_op jit(solution)/shard_map/squeeze | solution.py:115
  129.5 66.4 %while.18 = (s32[]{:T(128)}, f32[2,8,256]{2,1,0:T(8,128)S(1)}, f32[2,8,256]{2,1,0:T(8,128)S(1)}, f32[2,8,256,128]{3,2,1,0:T(8,128)}, s32[]{:T(128)}, /*index=5*/...) while((s32[]{:T(128)}, f32[2,8,256]{2,1,0:T(8,128)S(1)}, ...), condition=%wide.region_4.5_spmd.clone, body=%wide.region_1.4_spmd.clone.sunk | while | flops 2195216384 | bytes 73666816 | solution.py:60
  130.2 3.8 %bitcast_reduce_fusion.2 = (f32[2,8,256]{2,1,0:T(8,128)S(1)}, f32[2,1024,8,256]{3,1,2,0:T(8,128)S(1)}) fusion(pred[1024]{0:T(1024)(128)(4,1)S(1)} %add_compare_fusion.2, bf16[2,8,256,128]{3,2,1,0:T(8,128)(2,1)S(1)} %get-tuple-element.291, bf16[2,4096,128]{2,1,0:T(8,128)(2,1)} %get-tuple-element.290, s32[]{:T(128)S(6)} %select_n.67), kind=kOutput, calls=%fused_computation.1.clone.1 | convolution fusion | flops 1086320640 | bytes 18367492 | tf_op jit(solution)/shard_map/while/body/eval_jaxpr/kgrd,ksd->kgrs/dot_general | solution.py:37
  134.0 4.1 %fusion.61 = f32[2,8,256]{2,1,0:T(8,128)S(1)} fusion(f32[2,1024,8,256]{3,1,2,0:T(8,128)S(1)} %get-tuple-element.258, f32[2,8,256]{2,1,0:T(8,128)S(1)} %select_maximum_fusion.2, pred[1024]{0:T(1024)(128)(4,1)S(1)} %add_compare_fusion.2), kind=kLoop, calls=%fused_computation.5.clone.1 | loop fusion | flops 16773120 | bytes 16811008 | tf_op jit(solution)/shard_map/while/body/eval_jaxpr/reduce_sum | solution.py:52
  138.1 6.7 %fusion.63 = f32[2,8,256,128]{3,2,1,0:T(8,128)S(1)} fusion(f32[2,8,256,128]{3,2,1,0:T(8,128)S(1)} %copy-done.1, f32[2,1024,8,256]{3,1,2,0:T(8,128)S(1)} %get-tuple-element.258, f32[2,8,256]{2,1,0:T(8,128)S(1)} %select_maximum_fusion.2, pred[1024]{0:T(1024)(128)(4,1)S(1)} %add_compare_fusion.2, f32[2,8,256]{2,1,0:T(8,128)S(1)} %get-tuple-element.260, ...), kind=kOutput, calls=%fused_computation.9.clone.1 | convolution fusion | flops 1092091904 | bytes 21529604 | tf_op jit(solution)/shard_map/while/body/eval_jaxpr/kgrs,ksd->kgrd/dot_general | solution.py:45
  146.8 3.8 %bitcast_reduce_fusion.2 = (f32[2,8,256]{2,1,0:T(8,128)S(1)}, f32[2,1024,8,256]{3,1,2,0:T(8,128)S(1)}) fusion(pred[1024]{0:T(1024)(128)(4,1)S(1)} %add_compare_fusion.2, bf16[2,8,256,128]{3,2,1,0:T(8,128)(2,1)S(1)} %get-tuple-element.291, bf16[2,4096,128]{2,1,0:T(8,128)(2,1)} %get-tuple-element.290, s32[]{:T(128)S(6)} %select_n.67), kind=kOutput, calls=%fused_computation.1.clone.1 | convolution fusion | flops 1086320640 | bytes 18367492 | tf_op jit(solution)/shard_map/while/body/eval_jaxpr/kgrd,ksd->kgrs/dot_general | solution.py:37
  150.6 4.1 %fusion.61 = f32[2,8,256]{2,1,0:T(8,128)S(1)} fusion(f32[2,1024,8,256]{3,1,2,0:T(8,128)S(1)} %get-tuple-element.258, f32[2,8,256]{2,1,0:T(8,128)S(1)} %select_maximum_fusion.2, pred[1024]{0:T(1024)(128)(4,1)S(1)} %add_compare_fusion.2), kind=kLoop, calls=%fused_computation.5.clone.1 | loop fusion | flops 16773120 | bytes 16811008 | tf_op jit(solution)/shard_map/while/body/eval_jaxpr/reduce_sum | solution.py:52
  154.7 6.7 %fusion.63 = f32[2,8,256,128]{3,2,1,0:T(8,128)S(1)} fusion(f32[2,8,256,128]{3,2,1,0:T(8,128)S(1)} %copy-done.1, f32[2,1024,8,256]{3,1,2,0:T(8,128)S(1)} %get-tuple-element.258, f32[2,8,256]{2,1,0:T(8,128)S(1)} %select_maximum_fusion.2, pred[1024]{0:T(1024)(128)(4,1)S(1)} %add_compare_fusion.2, f32[2,8,256]{2,1,0:T(8,128)S(1)} %get-tuple-element.260, ...), kind=kOutput, calls=%fused_computation.9.clone.1 | convolution fusion | flops 1092091904 | bytes 21529604 | tf_op jit(solution)/shard_map/while/body/eval_jaxpr/kgrs,ksd->kgrd/dot_general | solution.py:45
  163.4 3.8 %bitcast_reduce_fusion.2 = (f32[2,8,256]{2,1,0:T(8,128)S(1)}, f32[2,1024,8,256]{3,1,2,0:T(8,128)S(1)}) fusion(pred[1024]{0:T(1024)(128)(4,1)S(1)} %add_compare_fusion.2, bf16[2,8,256,128]{3,2,1,0:T(8,128)(2,1)S(1)} %get-tuple-element.291, bf16[2,4096,128]{2,1,0:T(8,128)(2,1)} %get-tuple-element.290, s32[]{:T(128)S(6)} %select_n.67), kind=kOutput, calls=%fused_computation.1.clone.1 | convolution fusion | flops 1086320640 | bytes 18367492 | tf_op jit(solution)/shard_map/while/body/eval_jaxpr/kgrd,ksd->kgrs/dot_general | solution.py:37
  167.2 4.1 %fusion.61 = f32[2,8,256]{2,1,0:T(8,128)S(1)} fusion(f32[2,1024,8,256]{3,1,2,0:T(8,128)S(1)} %get-tuple-element.258, f32[2,8,256]{2,1,0:T(8,128)S(1)} %select_maximum_fusion.2, pred[1024]{0:T(1024)(128)(4,1)S(1)} %add_compare_fusion.2), kind=kLoop, calls=%fused_computation.5.clone.1 | loop fusion | flops 16773120 | bytes 16811008 | tf_op jit(solution)/shard_map/while/body/eval_jaxpr/reduce_sum | solution.py:52
  171.3 6.7 %fusion.63 = f32[2,8,256,128]{3,2,1,0:T(8,128)S(1)} fusion(f32[2,8,256,128]{3,2,1,0:T(8,128)S(1)} %copy-done.1, f32[2,1024,8,256]{3,1,2,0:T(8,128)S(1)} %get-tuple-element.258, f32[2,8,256]{2,1,0:T(8,128)S(1)} %select_maximum_fusion.2, pred[1024]{0:T(1024)(128)(4,1)S(1)} %add_compare_fusion.2, f32[2,8,256]{2,1,0:T(8,128)S(1)} %get-tuple-element.260, ...), kind=kOutput, calls=%fused_computation.9.clone.1 | convolution fusion | flops 1092091904 | bytes 21529604 | tf_op jit(solution)/shard_map/while/body/eval_jaxpr/kgrs,ksd->kgrd/dot_general | solution.py:45
  180.0 3.8 %bitcast_reduce_fusion.2 = (f32[2,8,256]{2,1,0:T(8,128)S(1)}, f32[2,1024,8,256]{3,1,2,0:T(8,128)S(1)}) fusion(pred[1024]{0:T(1024)(128)(4,1)S(1)} %add_compare_fusion.2, bf16[2,8,256,128]{3,2,1,0:T(8,128)(2,1)S(1)} %get-tuple-element.291, bf16[2,4096,128]{2,1,0:T(8,128)(2,1)} %get-tuple-element.290, s32[]{:T(128)S(6)} %select_n.67), kind=kOutput, calls=%fused_computation.1.clone.1 | convolution fusion | flops 1086320640 | bytes 18367492 | tf_op jit(solution)/shard_map/while/body/eval_jaxpr/kgrd,ksd->kgrs/dot_general | solution.py:37
  183.8 4.1 %fusion.61 = f32[2,8,256]{2,1,0:T(8,128)S(1)} fusion(f32[2,1024,8,256]{3,1,2,0:T(8,128)S(1)} %get-tuple-element.258, f32[2,8,256]{2,1,0:T(8,128)S(1)} %select_maximum_fusion.2, pred[1024]{0:T(1024)(128)(4,1)S(1)} %add_compare_fusion.2), kind=kLoop, calls=%fused_computation.5.clone.1 | loop fusion | flops 16773120 | bytes 16811008 | tf_op jit(solution)/shard_map/while/body/eval_jaxpr/reduce_sum | solution.py:52
  187.9 6.7 %fusion.63 = f32[2,8,256,128]{3,2,1,0:T(8,128)S(1)} fusion(f32[2,8,256,128]{3,2,1,0:T(8,128)S(1)} %copy-done.1, f32[2,1024,8,256]{3,1,2,0:T(8,128)S(1)} %get-tuple-element.258, f32[2,8,256]{2,1,0:T(8,128)S(1)} %select_maximum_fusion.2, pred[1024]{0:T(1024)(128)(4,1)S(1)} %add_compare_fusion.2, f32[2,8,256]{2,1,0:T(8,128)S(1)} %get-tuple-element.260, ...), kind=kOutput, calls=%fused_computation.9.clone.1 | convolution fusion | flops 1092091904 | bytes 21529604 | tf_op jit(solution)/shard_map/while/body/eval_jaxpr/kgrs,ksd->kgrd/dot_general | solution.py:45
  198.2 3.5 %all-to-all-start = ((f32[8,1,512]{2,1,0:T(1,128)}), f32[8,1,512]{2,1,0:T(1,128)S(1)}, u32[]{:S(2)}, u32[]{:S(2)}) async-start(f32[8,1,512]{2,1,0:T(1,128)} %reshape.106), calls=%async_computation | async-start | bytes 32768 | tf_op jit(solution)/shard_map/all_to_all | solution.py:118
  203.6 2.5 copy.73
  208.3 4.5 %all-to-all-start.1 = ((f32[1,256,16,128]{3,2,0,1:T(8,128)}), f32[1,256,16,128]{3,2,0,1:T(8,128)}, u32[]{:S(2)}, u32[]{:S(2)}) async-start(f32[1,256,16,128]{3,2,0,1:T(8,128)} %bitcast.114), calls=%async_computation.1 | async-start | bytes 4194304 | tf_op jit(solution)/shard_map/all_to_all | solution.py:119
  215.4 44.3 %all-to-all-done.1 = f32[1,256,16,128]{3,2,0,1:T(8,128)} async-done(((f32[1,256,16,128]{3,2,0,1:T(8,128)}), f32[1,256,16,128]{3,2,0,1:T(8,128)}, u32[]{:S(2)}, u32[]{:S(2)}) %all-to-all-start.1) | async-done | bytes 2097184 | tf_op jit(solution)/shard_map/all_to_all | solution.py:119
  265.4 2.9 collective-permute-done
  269.8 6.0 %collective-permute-done.1 = bf16[64,2048]{1,0:T(8,128)(2,1)S(1)} collective-permute-done((bf16[64,2048]{1,0:T(8,128)(2,1)S(1)}, bf16[64,2048]{1,0:T(8,128)(2,1)S(1)}, u32[]{:S(2)}, u32[]{:S(2)}) %collective-permute-start.1) | collective-permute-done | bytes 262176 | tf_op jit(solution)/shard_map/ppermute | solution.py:21
  276.3 23.8 %collective-permute-done.2 = bf16[128,2048]{1,0:T(8,128)(2,1)S(1)} collective-permute-done((bf16[128,2048]{1,0:T(8,128)(2,1)S(1)}, bf16[128,2048]{1,0:T(8,128)(2,1)S(1)}, u32[]{:S(2)}, u32[]{:S(2)}) %collective-permute-start.2) | collective-permute-done | bytes 524320 | tf_op jit(solution)/shard_map/ppermute | solution.py:21
  302.7 26.9 %reduce-scatter.2.cloned.1.call-done = f32[64,1024]{1,0:T(8,128)} async-done(((f32[256,1024]{1,0:T(8,128)}), f32[64,1024]{1,0:T(8,128)}) %reduce-scatter.2.cloned.1.call-update) | async-done | bytes 262160 | tf_op jit(solution)/shard_map/reduce_scatter | solution.py:135
  (89 shorter events, 32.7 us)
Async XLA Ops:
  6.5 1.5 copy-start
  134.0 4.1 %copy-start.1 = (f32[2,8,256,128]{3,2,1,0:T(8,128)S(1)}, f32[2,8,256,128]{3,2,1,0:T(8,128)}, u32[]{:S(2)}) copy-start(f32[2,8,256,128]{3,2,1,0:T(8,128)} %get-tuple-element.276) | copy-start | bytes 6291460 | tf_op jit(solution)/shard_map/while
  144.8 1.3 copy-start.2
  150.6 4.1 %copy-start.1 = (f32[2,8,256,128]{3,2,1,0:T(8,128)S(1)}, f32[2,8,256,128]{3,2,1,0:T(8,128)}, u32[]{:S(2)}) copy-start(f32[2,8,256,128]{3,2,1,0:T(8,128)} %get-tuple-element.276) | copy-start | bytes 6291460 | tf_op jit(solution)/shard_map/while
  161.4 1.3 copy-start.2
  167.2 4.1 %copy-start.1 = (f32[2,8,256,128]{3,2,1,0:T(8,128)S(1)}, f32[2,8,256,128]{3,2,1,0:T(8,128)}, u32[]{:S(2)}) copy-start(f32[2,8,256,128]{3,2,1,0:T(8,128)} %get-tuple-element.276) | copy-start | bytes 6291460 | tf_op jit(solution)/shard_map/while
  178.0 1.3 copy-start.2
  183.8 4.1 %copy-start.1 = (f32[2,8,256,128]{3,2,1,0:T(8,128)S(1)}, f32[2,8,256,128]{3,2,1,0:T(8,128)}, u32[]{:S(2)}) copy-start(f32[2,8,256,128]{3,2,1,0:T(8,128)} %get-tuple-element.276) | copy-start | bytes 6291460 | tf_op jit(solution)/shard_map/while
  194.6 1.3 copy-start.2
  198.2 10.1 %all-to-all-start = ((f32[8,1,512]{2,1,0:T(1,128)}), f32[8,1,512]{2,1,0:T(1,128)S(1)}, u32[]{:S(2)}, u32[]{:S(2)}) async-start(f32[8,1,512]{2,1,0:T(1,128)} %reshape.106), calls=%async_computation | async-start | bytes 32768 | tf_op jit(solution)/shard_map/all_to_all | solution.py:118
  208.3 4.8 %copy-start.3 = (s32[256]{0:T(256)S(1)}, s32[256]{0:T(256)}, u32[]{:S(2)}) copy-start(s32[256]{0:T(256)} %param.15) | copy-start | bytes 3076
  208.3 51.5 %all-to-all-start.1 = ((f32[1,256,16,128]{3,2,0,1:T(8,128)}), f32[1,256,16,128]{3,2,0,1:T(8,128)}, u32[]{:S(2)}, u32[]{:S(2)}) async-start(f32[1,256,16,128]{3,2,0,1:T(8,128)} %bitcast.114), calls=%async_computation.1 | async-start | bytes 4194304 | tf_op jit(solution)/shard_map/all_to_all | solution.py:119
  212.7 116.9 %reduce-scatter.2.cloned.1.call-start = ((), (), s32[]{:S(2)}) async-start(), calls=%async_computation.3 | async-start | bytes 1310720 | tf_op jit(solution)/shard_map/reduce_scatter | solution.py:135
  263.0 5.4 %collective-permute-start = (bf16[32,2048]{1,0:T(8,128)(2,1)S(1)}, bf16[32,2048]{1,0:T(8,128)(2,1)S(1)}, u32[]{:S(2)}, u32[]{:S(2)}) collective-permute-start(bf16[32,2048]{1,0:T(8,128)(2,1)S(1)} %copy_bitcast_fusion.1), channel_id=1, source_target_pairs={{0,28},{4,0},{8,4},{12,8},{16,12},{20,16},{24,20},{28,24},{1,29},{... | collective-permute-start | bytes 393224 | tf_op jit(solution)/shard_map/ppermute | solution.py:21
  268.4 7.4 %collective-permute-start.1 = (bf16[64,2048]{1,0:T(8,128)(2,1)S(1)}, bf16[64,2048]{1,0:T(8,128)(2,1)S(1)}, u32[]{:S(2)}, u32[]{:S(2)}) collective-permute-start(bf16[64,2048]{1,0:T(8,128)(2,1)S(1)} %pad_maximum_fusion.1), channel_id=1, source_target_pairs={{0,24},{4,28},{8,0},{12,4},{16,8},{20,12},{24,16},{28,20},{1,25},{... | collective-permute-start | bytes 786440 | tf_op jit(solution)/shard_map/ppermute | solution.py:21
  275.8 24.3 %collective-permute-start.2 = (bf16[128,2048]{1,0:T(8,128)(2,1)S(1)}, bf16[128,2048]{1,0:T(8,128)(2,1)S(1)}, u32[]{:S(2)}, u32[]{:S(2)}) collective-permute-start(bf16[128,2048]{1,0:T(8,128)(2,1)S(1)} %pad_maximum_fusion), channel_id=1, source_target_pairs={{0,16},{4,20},{8,24},{12,28},{16,0},{20,4},{24,8},{28,12},{1,17},{... | collective-permute-start | bytes 1572872 | tf_op jit(solution)/shard_map/ppermute | solution.py:21
  276.1 24.3 %copy-start.4 = (bf16[2048,1024]{1,0:T(8,128)(2,1)S(1)}, bf16[2048,1024]{1,0:T(8,128)(2,1)}, u32[]{:S(2)}) copy-start(bf16[2048,1024]{1,0:T(8,128)(2,1)} %param.12) | copy-start | bytes 12582916
Sparse Core Ops, SparseCore 0:
  302.8 26.7 reduce-scatter.1
